TPU v7x, 512 devices: a whole 4x4x16 slice. The times are simulated.
512 devices in a mesh: row: 16 (over y, x), col: 32 (over z, core).
Axes of the slice: x: 4, y: 4, z: 16, core: 2. Of those that a mesh axis runs over, the one named last changes fastest.
Arguments:
- momentum: float32 [4096, 14336], P('row', 'col'), may hold values from -6 to 6
- grads: bfloat16 [1, 4096, 14336], P(None, 'row', 'col'), may hold values from -6 to 6
- right_factor: float32 [128, 14336], P(None, 'col'), may hold values from -0.046875 to 0.046875
Outputs:
- new_momentum: float32 [4096, 14336], P('row', 'col')
- new_factor: float32 [128, 14336], P(None, 'col')
- update: float32 [4096, 14336], P('row', 'col')
All inputs are finite; a program needn't handle non-finite values.
Results may differ from a plain program's by a relative error of at most 0.0005.
Values sent between devices are 32-bit elements; how exact they have to be, the bound alone decides.
A program may use at most 64 MiB of HBM per device.

v0:
```python
import jax
import jax.numpy as jnp
from jax import lax
from jax.sharding import PartitionSpec as P

M = 4096
N = 14336
RANK = 128
POWER = 2
DECAY_LEFT = 0.05
EPSILON = 1e-06


def contract(first, second, first_dim, second_dim):
    return lax.dot_general(
        first,
        second,
        (((first_dim,), (second_dim,)), ((), ())),
        precision=lax.Precision.HIGHEST,
        preferred_element_type=jnp.float32,
    )


def orthonormal(gram_matrix, left_t):
    lower_f = jnp.linalg.cholesky(gram_matrix)
    return lax.linalg.triangular_solve(lower_f, left_t, left_side=True, lower=True)


def local(momentum, grads, right_factor):
    factor_t = right_factor
    moment = momentum
    blend = moment + grads[0].astype(jnp.float32)
    for sweep_index in range(POWER):
        partial_value = contract(factor_t, blend, 1, 1)
        left_t = lax.psum(partial_value, "col")
        gram_matrix = lax.psum(contract(left_t, left_t, 1, 1), "row")
        left_t = orthonormal(gram_matrix, left_t)
        right_t = lax.psum(contract(left_t, blend, 1, 0), "row")
        squares = lax.psum(jnp.sum(right_t * right_t, axis=1, keepdims=True), "col")
        factor_t = right_t / (jnp.sqrt(squares) + EPSILON)
    moment = blend - DECAY_LEFT * contract(left_t, right_t, 0, 0)
    accum = contract(left_t, factor_t, 0, 0)
    return (moment, factor_t, accum * jnp.float32((M * N / RANK) ** 0.5))


def solution(mesh):
    return jax.shard_map(
        local,
        mesh=mesh,
        in_specs=(P("row", "col"), P(None, "row", "col"), P(None, "col")),
        out_specs=(P("row", "col"), P(None, "col"), P("row", "col")),
        check_vma=False,
    )
```

profile of v0, /device:TPU:1, one launch (start us, length us, event | category | flops | bytes accessed | tf_op | source)
XLA Modules:
  0.0 1026.8 jit_solution(11263512012418945397)
XLA Ops:
  7.2 0.0 copy-start
  7.2 0.0 all-reduce.7.cloned.1.call-start
  7.2 0.9 copy-done
  8.1 2.7 convolution_bitcast_fusion
  10.8 0.0 all-reduce.7.cloned.1.call-update
  10.9 0.0 all-reduce.9.cloned.1.call-start
  10.9 204.7 %all-reduce.7.cloned.1.call-done = f32[128,256]{0,1:T(8,128)} async-done(((f32[128,256]{0,1:T(8,128)}), f32[128,256]{0,1:T(8,128)}) %all-reduce.7.cloned.1.call-update) | async-done | bytes 131088 | tf_op jit(solution)/shard_map/psum | solution.py:35
  215.6 2.0 fusion.16
  217.6 0.0 copy-start.1
  217.6 0.0 all-reduce.9.cloned.1.call-update
  217.6 0.0 all-reduce.11.cloned.1.call-start
  217.7 108.6 %all-reduce.9.cloned.1.call-done = f32[128,128]{0,1:T(8,128)} async-done(((f32[128,128]{0,1:T(8,128)}), f32[128,128]{0,1:T(8,128)}) %all-reduce.9.cloned.1.call-update) | async-done | bytes 65552 | tf_op jit(solution)/shard_map/psum | solution.py:36
  326.3 0.9 copy.7
  327.2 0.9 fusion.11
  328.1 0.0 copy-start.4
  328.1 11.7 %cholesky.44 = f32[128,128]{1,0:T(8,128)S(1)} custom-call(f32[128,128]{1,0:T(8,128)S(1)} %fusion.11), custom_call_target="Cholesky" | custom-call | tf_op jit(solution)/shard_map/jit(cholesky)/cholesky | solution.py:25
  339.8 0.6 compare_reduce_fusion.1
  340.5 0.0 copy-start.2
  340.5 0.7 fusion.4
  341.2 9.8 custom-call.6
  351.0 0.0 copy-done.4
  351.0 0.3 fusion.9
  351.3 0.0 copy-done.1
  351.3 0.0 copy-done.2
  351.3 1.2 fusion.15
  352.6 0.0 all-reduce.11.cloned.1.call-update
  352.6 0.0 all-reduce.13.cloned.1.call-start
  352.6 115.1 %all-reduce.11.cloned.1.call-done = f32[128,448]{0,1:T(8,128)} async-done(((f32[128,448]{0,1:T(8,128)}), f32[128,448]{0,1:T(8,128)}) %all-reduce.11.cloned.1.call-update) | async-done | bytes 229392 | tf_op jit(solution)/shard_map/psum | solution.py:38
  467.7 0.0 copy-start.8
  467.7 1.1 multiply_reduce_fusion.1
  468.8 48.9 %psum.59 = f32[128,1]{0,1:T(1,128)S(1)} all-reduce(f32[128,1]{0,1:T(1,128)S(1)} %bitcast.48), channel_id=1, replica_groups=mesh['row'=16,'col'=32] {'col'}, use_global_device_ids=true, to_apply=%region_6.9 | all-reduce | flops 128 | bytes 1024 | tf_op jit(solution)/shard_map/psum | solution.py:39
  517.7 0.0 copy-done.8
  517.7 1.3 fusion.1
  519.0 0.0 all-reduce.13.cloned.1.call-update
  519.0 0.0 all-reduce.15.cloned.1.call-start
  519.1 197.1 %all-reduce.13.cloned.1.call-done = f32[128,256]{1,0:T(8,128)} async-done(((f32[128,256]{1,0:T(8,128)}), f32[128,256]{1,0:T(8,128)}) %all-reduce.13.cloned.1.call-update) | async-done | bytes 131088 | tf_op jit(solution)/shard_map/psum | solution.py:35
  716.2 1.9 fusion.17
  718.0 0.0 all-reduce.15.cloned.1.call-update
  718.1 0.2 all-reduce.17.cloned.1.call-start
  718.3 108.4 %all-reduce.15.cloned.1.call-done = f32[128,128]{0,1:T(8,128)} async-done(((f32[128,128]{0,1:T(8,128)}), f32[128,128]{0,1:T(8,128)}) %all-reduce.15.cloned.1.call-update) | async-done | bytes 65552 | tf_op jit(solution)/shard_map/psum | solution.py:36
  826.7 0.0 copy-start.7
  826.7 1.0 copy.9
  827.7 0.0 copy-done.7
  827.7 0.0 copy-start.5
  827.8 11.7 %cholesky.55 = f32[128,128]{1,0:T(8,128)S(1)} custom-call(f32[128,128]{1,0:T(8,128)S(1)} %fusion.8), custom_call_target="Cholesky" | custom-call | tf_op jit(solution)/shard_map/jit(cholesky)/cholesky | solution.py:25
  839.5 0.6 compare_reduce_fusion
  840.1 0.7 fusion.5
  840.8 9.8 custom-call.7
  850.6 0.0 copy-done.5
  850.6 0.3 fusion.6
  850.9 1.2 fusion.14
  852.2 0.0 all-reduce.17.cloned.1.call-update
  852.2 115.1 %all-reduce.17.cloned.1.call-done = f32[128,448]{0,1:T(8,128)} async-done(((f32[128,448]{0,1:T(8,128)}), f32[128,448]{0,1:T(8,128)}) %all-reduce.17.cloned.1.call-update) | async-done | bytes 229392 | tf_op jit(solution)/shard_map/psum | solution.py:38
  967.3 0.0 copy-start.3
  967.3 1.1 multiply_reduce_fusion
  968.4 48.9 %psum.63 = f32[128,1]{0,1:T(1,128)S(1)} all-reduce(f32[128,1]{0,1:T(1,128)S(1)} %bitcast.49), channel_id=1, replica_groups=mesh['row'=16,'col'=32] {'col'}, use_global_device_ids=true, to_apply=%region_11.14 | all-reduce | flops 128 | bytes 1024 | tf_op jit(solution)/shard_map/psum | solution.py:39
  1017.3 0.0 copy-done.3
  1017.4 0.0 copy-start.6
  1017.4 1.3 convolution_multiply_fusion
  1018.7 0.0 copy-done.6
  1018.7 1.3 fusion
  (6 shorter events, 0.1 us)
Async XLA Ops:
  7.2 0.9 copy-start
  7.2 208.4 %all-reduce.7.cloned.1.call-start = ((), (), s32[]{:S(2)}) async-start(), calls=%async_computation | async-start | bytes 262144 | tf_op jit(solution)/shard_map/psum | solution.py:35
  10.9 315.4 %all-reduce.9.cloned.1.call-start = ((), (), s32[]{:S(2)}) async-start(), calls=%async_computation.1 | async-start | bytes 131072 | tf_op jit(solution)/shard_map/psum | solution.py:36
  217.6 133.7 %copy-start.1 = (f32[256,448]{0,1:T(8,128)S(1)}, f32[256,448]{0,1:T(8,128)}, u32[]{:S(2)}) copy-start(f32[256,448]{0,1:T(8,128)} %param.6) | copy-start | bytes 1376260
  217.6 250.1 %all-reduce.11.cloned.1.call-start = ((), (), s32[]{:S(2)}) async-start(), calls=%async_computation.2 | async-start | bytes 458752 | tf_op jit(solution)/shard_map/psum | solution.py:38
  328.1 22.9 %copy-start.4 = (f32[128,256]{0,1:T(8,128)S(1)}, f32[128,256]{0,1:T(8,128)}, u32[]{:S(2)}) copy-start(f32[128,256]{0,1:T(8,128)} %all-reduce.7.cloned.1.call-done) | copy-start | bytes 393220
  340.5 10.9 %copy-start.2 = (bf16[1,256,448]{1,2,0:T(8,128)(2,1)S(1)}, bf16[1,256,448]{1,2,0:T(8,128)(2,1)}, u32[]{:S(2)}) copy-start(bf16[1,256,448]{1,2,0:T(8,128)(2,1)} %param.7) | copy-start | bytes 688132
  352.6 363.6 %all-reduce.13.cloned.1.call-start = ((), (), s32[]{:S(2)}) async-start(), calls=%async_computation.3 | async-start | bytes 262144 | tf_op jit(solution)/shard_map/psum | solution.py:35
  467.7 50.0 %copy-start.8 = (f32[128,448]{0,1:T(8,128)S(1)}, f32[128,448]{0,1:T(8,128)}, u32[]{:S(2)}) copy-start(f32[128,448]{0,1:T(8,128)} %all-reduce.11.cloned.1.call-done) | copy-start | bytes 688132
  519.0 307.7 %all-reduce.15.cloned.1.call-start = ((), (), s32[]{:S(2)}) async-start(), calls=%async_computation.4 | async-start | bytes 131072 | tf_op jit(solution)/shard_map/psum | solution.py:36
  718.1 249.3 %all-reduce.17.cloned.1.call-start = ((), (), s32[]{:S(2)}) async-start(), calls=%async_computation.5 | async-start | bytes 458752 | tf_op jit(solution)/shard_map/psum | solution.py:38
  826.7 1.0 copy-start.7
  827.7 22.9 %copy-start.5 = (f32[128,256]{1,0:T(8,128)S(1)}, f32[128,256]{1,0:T(8,128)}, u32[]{:S(2)}) copy-start(f32[128,256]{1,0:T(8,128)} %all-reduce.13.cloned.1.call-done) | copy-start | bytes 393220
  967.3 50.0 %copy-start.3 = (f32[128,448]{0,1:T(8,128)S(1)}, f32[128,448]{0,1:T(8,128)}, u32[]{:S(2)}) copy-start(f32[128,448]{0,1:T(8,128)} %all-reduce.17.cloned.1.call-done) | copy-start | bytes 688132
  1017.4 1.3 copy-start.6
Sparse Core Ops, SparseCore 0:
  11.0 204.5 all-reduce.6
  219.3 106.8 all-reduce.8
  352.7 114.9 all-reduce.10
  519.1 196.9 all-reduce.12
  719.8 106.8 all-reduce.14
  852.3 114.9 all-reduce.16
where the time goes:
time: 1030 us
  waiting for transfers between devices  849 us (82%)
  blocking collectives  97.8 us (9%)
  other arithmetic  48.8 us (5%)
  between operations  14.3 us (1%)
  matrix products  13.5 us (1%)
    psum x2, waiting for transfers between devices, local(): left_t = lax.psum(partial_value, 'col')  402 us
    psum x2, waiting for transfers between devices, local(): right_t = lax.psum(contract(left_t, blend, 1, 0), 'row')  230 us
    psum x2, waiting for transfers between devices, local(): gram_matrix = lax.psum(contract(left_t, left_t, 1, 1), 'row')  217 us
    psum x2, blocking collectives, local(): squares = lax.psum(jnp.sum(right_t * right_t, axis=1, keepdims=True), 'col')  97.8 us
    another operation x6, other arithmetic, orthonormal(): lower_f = jnp.linalg.cholesky(gram_matrix)  24.8 us
    another operation x4, other arithmetic, orthonormal(): lax.linalg.triangular_solve(lower_f, left_t, left_side=True, lower=True)  21 us
  transfers between devices with their start and end apart: 6, of which 6 were waited for; matrix products, arithmetic and copies ran while one was open for 0% of the time, Pallas kernels for 0%

commit v1 on v0

--- a/solution.py
+++ b/solution.py
@@ -36,7 +36,9 @@
         gram_matrix = lax.psum(contract(left_t, left_t, 1, 1), "row")
         left_t = orthonormal(gram_matrix, left_t)
         right_t = lax.psum(contract(left_t, blend, 1, 0), "row")
-        squares = lax.psum(jnp.sum(right_t * right_t, axis=1, keepdims=True), "col")
+        block = jnp.sum(right_t * right_t, axis=1, keepdims=True)
+        parts = lax.all_gather(block, "col", axis=0, tiled=False)
+        squares = parts.sum(axis=0)
         factor_t = right_t / (jnp.sqrt(squares) + EPSILON)
     moment = blend - DECAY_LEFT * contract(left_t, right_t, 0, 0)
     accum = contract(left_t, factor_t, 0, 0)

time: 1030 us -> 994 us (0.965)
  blocking collectives: 97.8 us -> 66.9 us
    psum x2 -> x0, blocking collectives: 97.8 us -> none  [local(): squares = lax.psum(jnp.sum(right_t * right_t, axis=1, keepdims=True), 'col')]
    all_gather x0 -> x2, blocking collectives: none -> 66.9 us  [local(): parts = lax.all_gather(block, 'col', axis=0, tiled=False)]
where the time goes in v1:
time: 994 us; the launch traced here: 993 us
  waiting for transfers between devices  846 us (85%)
  blocking collectives  66.9 us (7%)
  other arithmetic  48.9 us (5%)
  between operations  14.3 us (1%)
  matrix products  13.5 us (1%)
    psum x2, waiting for transfers between devices, local(): left_t = lax.psum(partial_value, 'col')  399 us
    psum x2, waiting for transfers between devices, local(): right_t = lax.psum(contract(left_t, blend, 1, 0), 'row')  230 us
    psum x2, waiting for transfers between devices, local(): gram_matrix = lax.psum(contract(left_t, left_t, 1, 1), 'row')  217 us
    all_gather x2, blocking collectives, local(): parts = lax.all_gather(block, 'col', axis=0, tiled=False)  66.9 us
    another operation x6, other arithmetic, orthonormal(): lower_f = jnp.linalg.cholesky(gram_matrix)  24.8 us
    another operation x4, other arithmetic, orthonormal(): lax.linalg.triangular_solve(lower_f, left_t, left_side=True, lower=True)  21 us
  transfers between devices with their start and end apart: 6, of which 6 were waited for; matrix products, arithmetic and copies ran while one was open for 0% of the time, Pallas kernels for 0%

profile of v1, /device:TPU:1, one launch (start us, length us, event | category | flops | bytes accessed | tf_op | source)
XLA Modules:
  0.0 993.2 jit_solution(5063787613403649436)
XLA Ops:
  7.2 0.0 copy-start
  7.2 0.0 all-reduce.7.cloned.1.call-start
  7.2 0.9 copy-done
  8.1 2.7 convolution_bitcast_fusion
  10.8 0.0 all-reduce.7.cloned.1.call-update
  10.9 0.0 all-reduce.9.cloned.1.call-start
  10.9 204.7 %all-reduce.7.cloned.1.call-done = f32[128,256]{0,1:T(8,128)} async-done(((f32[128,256]{0,1:T(8,128)}), f32[128,256]{0,1:T(8,128)}) %all-reduce.7.cloned.1.call-update) | async-done | bytes 131088 | tf_op jit(solution)/shard_map/psum | solution.py:35
  215.6 2.0 fusion.16
  217.6 0.0 copy-start.1
  217.6 0.0 all-reduce.9.cloned.1.call-update
  217.6 0.0 all-reduce.11.cloned.1.call-start
  217.7 108.6 %all-reduce.9.cloned.1.call-done = f32[128,128]{0,1:T(8,128)} async-done(((f32[128,128]{0,1:T(8,128)}), f32[128,128]{0,1:T(8,128)}) %all-reduce.9.cloned.1.call-update) | async-done | bytes 65552 | tf_op jit(solution)/shard_map/psum | solution.py:36
  326.3 0.9 copy.11
  327.2 0.9 fusion.11
  328.1 0.0 copy-start.4
  328.1 11.7 %cholesky.44 = f32[128,128]{1,0:T(8,128)S(1)} custom-call(f32[128,128]{1,0:T(8,128)S(1)} %fusion.11), custom_call_target="Cholesky" | custom-call | tf_op jit(solution)/shard_map/jit(cholesky)/cholesky | solution.py:25
  339.8 0.6 compare_reduce_fusion.1
  340.5 0.0 copy-start.2
  340.5 0.7 fusion.4
  341.2 9.8 custom-call.6
  351.0 0.0 copy-done.4
  351.0 0.3 fusion.9
  351.3 0.0 copy-done.1
  351.3 0.0 copy-done.2
  351.3 1.2 fusion.15
  352.6 0.0 all-reduce.11.cloned.1.call-update
  352.6 0.0 all-reduce.13.cloned.1.call-start
  352.6 115.1 %all-reduce.11.cloned.1.call-done = f32[128,448]{0,1:T(8,128)} async-done(((f32[128,448]{0,1:T(8,128)}), f32[128,448]{0,1:T(8,128)}) %all-reduce.11.cloned.1.call-update) | async-done | bytes 229392 | tf_op jit(solution)/shard_map/psum | solution.py:38
  467.7 0.0 copy-start.8
  467.7 1.1 multiply_reduce_fusion.1
  468.8 33.4 %all-gather.2 = f32[32,1,128]{2,1,0:T(1,128)S(1)} all-gather(f32[1,1,128]{2,1,0:T(1,128)S(1)} %bitcast.44), channel_id=2, replica_groups=mesh['row'=16,'col'=32] {'col'}, dimensions={0}, use_global_device_ids=true | all-gather | bytes 16896 | tf_op jit(solution)/shard_map/all_gather | solution.py:40
  502.2 0.1 reduce.6
  502.3 0.0 copy-done.8
  502.3 1.3 fusion.1
  503.6 0.0 all-reduce.13.cloned.1.call-update
  503.6 0.0 all-reduce.15.cloned.1.call-start
  503.6 194.3 %all-reduce.13.cloned.1.call-done = f32[128,256]{1,0:T(8,128)} async-done(((f32[128,256]{1,0:T(8,128)}), f32[128,256]{1,0:T(8,128)}) %all-reduce.13.cloned.1.call-update) | async-done | bytes 131088 | tf_op jit(solution)/shard_map/psum | solution.py:35
  698.0 1.9 fusion.17
  699.9 0.0 all-reduce.15.cloned.1.call-update
  699.9 0.2 all-reduce.17.cloned.1.call-start
  700.1 108.4 %all-reduce.15.cloned.1.call-done = f32[128,128]{0,1:T(8,128)} async-done(((f32[128,128]{0,1:T(8,128)}), f32[128,128]{0,1:T(8,128)}) %all-reduce.15.cloned.1.call-update) | async-done | bytes 65552 | tf_op jit(solution)/shard_map/psum | solution.py:36
  808.5 0.0 copy-start.7
  808.5 1.0 copy.13
  809.5 0.0 copy-done.7
  809.6 0.0 copy-start.5
  809.6 11.7 %cholesky.55 = f32[128,128]{1,0:T(8,128)S(1)} custom-call(f32[128,128]{1,0:T(8,128)S(1)} %fusion.8), custom_call_target="Cholesky" | custom-call | tf_op jit(solution)/shard_map/jit(cholesky)/cholesky | solution.py:25
  821.3 0.6 compare_reduce_fusion
  822.0 0.7 fusion.5
  822.6 9.8 custom-call.7
  832.4 0.0 copy-done.5
  832.4 0.3 fusion.6
  832.8 1.2 fusion.14
  834.0 0.0 all-reduce.17.cloned.1.call-update
  834.0 115.1 %all-reduce.17.cloned.1.call-done = f32[128,448]{0,1:T(8,128)} async-done(((f32[128,448]{0,1:T(8,128)}), f32[128,448]{0,1:T(8,128)}) %all-reduce.17.cloned.1.call-update) | async-done | bytes 229392 | tf_op jit(solution)/shard_map/psum | solution.py:38
  949.1 0.0 copy-start.3
  949.2 1.1 multiply_reduce_fusion
  950.2 33.4 %all-gather.3 = f32[32,1,128]{2,1,0:T(1,128)S(1)} all-gather(f32[1,1,128]{2,1,0:T(1,128)S(1)} %bitcast.45), channel_id=3, replica_groups=mesh['row'=16,'col'=32] {'col'}, dimensions={0}, use_global_device_ids=true | all-gather | bytes 16896 | tf_op jit(solution)/shard_map/all_gather | solution.py:40
  983.7 0.1 reduce.7
  983.7 0.0 copy-done.3
  983.8 0.0 copy-start.6
  983.8 1.3 convolution_multiply_fusion
  985.1 0.0 copy-done.6
  985.1 1.3 fusion
  (6 shorter events, 0.1 us)
Async XLA Ops:
  7.2 0.9 copy-start
  7.2 208.4 %all-reduce.7.cloned.1.call-start = ((), (), s32[]{:S(2)}) async-start(), calls=%async_computation | async-start | bytes 262144 | tf_op jit(solution)/shard_map/psum | solution.py:35
  10.9 315.4 %all-reduce.9.cloned.1.call-start = ((), (), s32[]{:S(2)}) async-start(), calls=%async_computation.1 | async-start | bytes 131072 | tf_op jit(solution)/shard_map/psum | solution.py:36
  217.6 133.7 %copy-start.1 = (f32[256,448]{0,1:T(8,128)S(1)}, f32[256,448]{0,1:T(8,128)}, u32[]{:S(2)}) copy-start(f32[256,448]{0,1:T(8,128)} %param.6) | copy-start | bytes 1376260
  217.6 250.1 %all-reduce.11.cloned.1.call-start = ((), (), s32[]{:S(2)}) async-start(), calls=%async_computation.2 | async-start | bytes 458752 | tf_op jit(solution)/shard_map/psum | solution.py:38
  328.1 22.9 %copy-start.4 = (f32[128,256]{0,1:T(8,128)S(1)}, f32[128,256]{0,1:T(8,128)}, u32[]{:S(2)}) copy-start(f32[128,256]{0,1:T(8,128)} %all-reduce.7.cloned.1.call-done) | copy-start | bytes 393220
  340.5 10.9 %copy-start.2 = (bf16[1,256,448]{1,2,0:T(8,128)(2,1)S(1)}, bf16[1,256,448]{1,2,0:T(8,128)(2,1)}, u32[]{:S(2)}) copy-start(bf16[1,256,448]{1,2,0:T(8,128)(2,1)} %param.7) | copy-start | bytes 688132
  352.6 345.4 %all-reduce.13.cloned.1.call-start = ((), (), s32[]{:S(2)}) async-start(), calls=%async_computation.3 | async-start | bytes 262144 | tf_op jit(solution)/shard_map/psum | solution.py:35
  467.7 34.6 %copy-start.8 = (f32[128,448]{0,1:T(8,128)S(1)}, f32[128,448]{0,1:T(8,128)}, u32[]{:S(2)}) copy-start(f32[128,448]{0,1:T(8,128)} %all-reduce.11.cloned.1.call-done) | copy-start | bytes 688132
  503.6 304.9 %all-reduce.15.cloned.1.call-start = ((), (), s32[]{:S(2)}) async-start(), calls=%async_computation.4 | async-start | bytes 131072 | tf_op jit(solution)/shard_map/psum | solution.py:36
  699.9 249.3 %all-reduce.17.cloned.1.call-start = ((), (), s32[]{:S(2)}) async-start(), calls=%async_computation.5 | async-start | bytes 458752 | tf_op jit(solution)/shard_map/psum | solution.py:38
  808.5 1.0 copy-start.7
  809.6 22.9 %copy-start.5 = (f32[128,256]{1,0:T(8,128)S(1)}, f32[128,256]{1,0:T(8,128)}, u32[]{:S(2)}) copy-start(f32[128,256]{1,0:T(8,128)} %all-reduce.13.cloned.1.call-done) | copy-start | bytes 393220
  949.1 34.6 %copy-start.3 = (f32[128,448]{0,1:T(8,128)S(1)}, f32[128,448]{0,1:T(8,128)}, u32[]{:S(2)}) copy-start(f32[128,448]{0,1:T(8,128)} %all-reduce.17.cloned.1.call-done) | copy-start | bytes 688132
  983.8 1.3 copy-start.6
Sparse Core Ops, SparseCore 0:
  11.0 204.5 all-reduce.6
  219.3 106.8 all-reduce.8
  352.7 114.9 all-reduce.10
  503.7 194.2 all-reduce.12
  701.6 106.8 all-reduce.14
  834.1 114.9 all-reduce.16
